TPU v7x, 256 devices: a whole 4x4x8 slice. The times are simulated.
256 devices in a mesh: narrow: 8 (over y, z_lo), wide: 8 (over z_hi, core), nys: 4 (over x).
Axes of the slice: x: 4, y: 4, z: 8 (z_hi: 4, z_lo: 2; z = z_hi * 2 + z_lo), core: 2. Of those that a mesh axis runs over, the one named last changes fastest.
Arguments:
- centers: bfloat16 [262144, 1024], P(('narrow', 'wide', 'nys')), may hold values from -6 to 6
- weights: float32 [262144, 1000], P(('narrow', 'wide', 'nys')), may hold values from -6 to 6
- batch_points: bfloat16 [512, 1024], P(('narrow', 'wide', 'nys')), may hold values from -6 to 6
- labels: float32 [512, 1000], P(('narrow', 'wide', 'nys')), may hold values from -6 to 6
- nystrom_points: bfloat16 [2048, 1024], P(('narrow', 'nys')), may hold values from -6 to 6
- eigvecs: float32 [2048, 160], P(('narrow', 'nys')), may hold values from -0.125 to 0.125
- corrections: float32 [160], replicated, may hold values from 0.05 to 0.5
Outputs:
- new_weights: float32 [262144, 1000], P(('narrow', 'wide', 'nys'))
All inputs are finite; a program needn't handle non-finite values.
Results may differ from a plain program's by a relative error of at most 0.0003.
The roundings to bfloat16 on the way count: a program that leaves them out, or rounds other values in their place, can miss the bound.
Values may be sent and summed in bfloat16 or wider, within the bound.
A program may use at most 64 MiB of HBM per device.

v0:
```python
import math
import jax
import jax.numpy as jnp
from jax import lax
from jax.sharding import PartitionSpec as P

BATCH = 512
RATE = 16.0
SPREAD = 4.0


def kernel_with(left, left_sq, right):
    cross = lax.dot_general(
        left, right, (((1,), (1,)), ((), ())), preferred_element_type=jnp.float32
    )
    right_sq = jnp.sum(jnp.square(right.astype(jnp.float32)), axis=1)
    dist = jnp.sqrt(jnp.maximum(left_sq[:, None] + right_sq[None, :] - 2.0 * cross, 0.0))
    radius = math.sqrt(2.0 * left.shape[1])
    return jnp.exp((radius - dist) / SPREAD).astype(jnp.bfloat16)


def squares(points):
    return jnp.sum(jnp.square(points.astype(jnp.float32)), axis=1)


def per_device(centers, weights, batch_points, labels, nystrom_points, eigvecs, corrections):
    batch_all = lax.all_gather(batch_points, ("narrow", "wide", "nys"), axis=0, tiled=True)
    count = lax.axis_size(("narrow", "wide", "nys"))
    scale = (centers.shape[0] * count) ** (-0.5)
    center_sq = squares(centers)
    k_batch = kernel_with(centers, center_sq, batch_all)
    partial_value = (
        lax.dot_general(
            k_batch,
            weights.astype(jnp.bfloat16),
            (((0,), (0,)), ((), ())),
            preferred_element_type=jnp.float32,
        )
        * scale
    )
    rows = labels.shape[0]
    offset = lax.axis_index(("narrow", "wide", "nys")) * rows
    placed = lax.dynamic_update_slice(jnp.zeros_like(partial_value), labels, (offset, jnp.int32(0)))
    residual = lax.psum(partial_value - placed, ("narrow", "wide", "nys")).astype(jnp.bfloat16)
    k_nystrom = kernel_with(nystrom_points, squares(nystrom_points), batch_all)
    pulled = jnp.dot(k_nystrom, residual, preferred_element_type=jnp.float32)
    local_proj = lax.dot_general(
        eigvecs, pulled, (((0,), (0,)), ((), ())), precision=lax.Precision.HIGHEST
    )
    projected = lax.psum(local_proj, ("narrow", "nys"))
    scaled_proj = corrections[:, None] * projected
    gradient = jnp.dot(k_batch, residual, preferred_element_type=jnp.float32)
    corrected = jnp.dot(eigvecs, scaled_proj, precision=lax.Precision.HIGHEST).astype(jnp.bfloat16)
    points = lax.all_gather(nystrom_points, ("narrow", "nys"), axis=0, tiled=True)
    coefs = lax.all_gather(corrected, ("narrow", "nys"), axis=0, tiled=True)
    tile = kernel_with(centers, center_sq, points)
    nystrom_term = jnp.dot(tile, coefs, preferred_element_type=jnp.float32)
    return weights - RATE / BATCH * (gradient - nystrom_term)


def solution(mesh):
    placed = (
        P(("narrow", "wide", "nys"), None),
        P(("narrow", "wide", "nys"), None),
        P(("narrow", "wide", "nys"), None),
        P(("narrow", "wide", "nys"), None),
        P(("narrow", "nys"), None),
        P(("narrow", "nys"), None),
        P(),
    )
    return jax.shard_map(
        per_device,
        mesh=mesh,
        in_specs=placed,
        out_specs=P(("narrow", "wide", "nys"), None),
        check_vma=False,
    )
```

profile of v0, /device:TPU:2, one launch (start us, length us, event | category | flops | bytes accessed | tf_op | source)
XLA Modules:
  0.0 1286.6 jit_solution(18334620316952581570)
XLA Ops:
  6.5 0.0 copy-start
  6.5 0.0 all-gather.9.cloned.1.call-start
  6.5 0.7 all-gather.9.cloned.1.call-update
  7.3 0.0 all-reduce.3.cloned.1.call-start
  7.3 0.9 copy.9
  8.2 0.2 broadcast_in_dim.2
  8.5 6.3 dynamic_update_slice.3
  14.8 1.0 multiply_reduce_fusion.3
  15.8 2.1 multiply_reduce_fusion.1
  17.9 523.6 %all-gather.9.cloned.1.call-done = bf16[256,2,1024]{2,1,0:T(2,128)(2,1)} async-done(((bf16[1,2,1024]{2,1,0:T(2,128)(2,1)}), bf16[256,2,1024]{2,1,0:T(2,128)(2,1)}) %all-gather.9.cloned.1.call-update) | async-done | bytes 1048592 | tf_op jit(solution)/shard_map/all_gather | solution.py:27
  541.5 1.5 reshape.6
  543.0 0.3 multiply_reduce_fusion.2
  543.3 0.0 copy-start.1
  543.3 3.8 exponential_convert_fusion.1
  547.1 0.0 copy-start.2
  547.1 1.1 copy-done.2
  548.2 0.0 copy-done.1
  548.2 0.0 copy-start.4
  548.2 2.6 multiply_subtract_fusion.1
  550.7 0.0 copy-start.5
  550.7 81.6 %all-reduce.4 = bf16[512,1000]{0,1:T(8,128)(2,1)S(1)} all-reduce(f32[512,1000]{0,1:T(8,128)} %multiply_subtract_fusion.1), channel_id=1, replica_groups=mesh['narrow'=8,'wide'=8,'nys'=4] {'narrow','wide','nys'}, use_global_device_ids=true, to_apply=%region_2.0 | all-reduce | flops 512000 | bytes 3072000 | tf_op jit(solution)/shard_map/psum | solution.py:44
  632.3 0.0 copy-done.4
  632.3 0.8 fusion.12
  633.2 0.0 copy-done
  633.2 1.6 convolution_bitcast_fusion
  634.7 0.0 all-reduce.3.cloned.1.call-update
  634.7 0.0 all-gather.5.cloned.1.call-start
  634.8 0.7 all-gather.5.cloned.1.call-update
  635.5 0.2 all-gather.7.cloned.1.call-start
  635.7 301.3 %all-reduce.3.cloned.1.call-done = f32[160,1000]{1,0:T(8,128)} async-done(((f32[160,1000]{1,0:T(8,128)}), f32[160,1000]{1,0:T(8,128)}) %all-reduce.3.cloned.1.call-update) | async-done | bytes 640016 | tf_op jit(solution)/shard_map/psum | solution.py:50
  937.0 0.0 copy-done.5
  937.0 2.3 fusion.4
  939.4 0.0 all-gather.7.cloned.1.call-update
  939.4 157.5 %all-gather.5.cloned.1.call-done = bf16[2048,1024]{1,0:T(8,128)(2,1)} async-done(((bf16[64,1024]{1,0:T(8,128)(2,1)}), bf16[2048,1024]{1,0:T(8,128)(2,1)}) %all-gather.5.cloned.1.call-update) | async-done | bytes 4194320 | tf_op jit(solution)/shard_map/all_gather | solution.py:54
  1097.0 3.1 multiply_reduce_fusion
  1100.0 0.0 copy-start.3
  1100.1 157.9 %all-gather.7.cloned.1.call-done = bf16[2048,1000]{1,0:T(8,128)(2,1)} async-done(((bf16[64,1000]{1,0:T(8,128)(2,1)}), bf16[2048,1000]{1,0:T(8,128)(2,1)}) %all-gather.7.cloned.1.call-update) | async-done | bytes 4096016 | tf_op jit(solution)/shard_map/all_gather | solution.py:55
  1258.0 15.5 %fusion.13 = f32[1024,1000]{0,1:T(8,128)} fusion(bf16[2048,1000]{1,0:T(8,128)(2,1)} %all-gather.7.cloned.1.call-done, bf16[1024,1024]{1,0:T(8,128)(2,1)} %param.7, bf16[2048,1024]{1,0:T(8,128)(2,1)} %all-gather.5.cloned.1.call-done, f32[2048]{0:T(1024)S(1)} %multiply_reduce_fusion, f32[1024]{0:T(1024)S(1)} %multiply_reduce_fusion.1), kind=kOutput, calls=%fused_computation.21 | convolution fusion | flops 8503951360 | bytes 14495744 | tf_op jit(solution)/shard_map/dot_general | solution.py:57
  1273.5 0.0 copy-done.3
  1273.5 6.7 multiply_subtract_fusion
Async XLA Ops:
  6.5 626.6 %copy-start = (f32[64,160]{1,0:T(8,128)S(1)}, f32[64,160]{1,0:T(8,128)}, u32[]{:S(2)}) copy-start(f32[64,160]{1,0:T(8,128)} %param.12) | copy-start | bytes 122884
  6.5 535.0 %all-gather.9.cloned.1.call-start = ((), (), s32[]{:S(2)}) async-start(), calls=%async_computation.3 | async-start | bytes 1052672 | tf_op jit(solution)/shard_map/all_gather | solution.py:27
  7.3 929.8 %all-reduce.3.cloned.1.call-start = ((), (), s32[]{:S(2)}) async-start(), calls=%async_computation.1 | async-start | bytes 1310720 | tf_op jit(solution)/shard_map/psum | solution.py:50
  543.3 4.9 copy-start.1
  547.1 1.1 copy-start.2
  548.2 84.1 %copy-start.4 = (bf16[64,1024]{1,0:T(8,128)(2,1)S(1)}, bf16[64,1024]{1,0:T(8,128)(2,1)}, u32[]{:S(2)}) copy-start(bf16[64,1024]{1,0:T(8,128)(2,1)} %param.11) | copy-start | bytes 393220
  550.7 386.3 %copy-start.5 = (f32[160]{0:T(256)S(1)}, f32[160]{0:T(256)}, u32[]{:S(2)}) copy-start(f32[160]{0:T(256)} %param.13) | copy-start | bytes 1924
  634.7 462.2 %all-gather.5.cloned.1.call-start = ((), (), s32[]{:S(2)}) async-start(), calls=%async_computation | async-start | bytes 4325376 | tf_op jit(solution)/shard_map/all_gather | solution.py:54
  635.5 622.5 %all-gather.7.cloned.1.call-start = ((), (), s32[]{:S(2)}) async-start(), calls=%async_computation.2 | async-start | bytes 4325376 | tf_op jit(solution)/shard_map/all_gather | solution.py:55
  1100.0 173.4 %copy-start.3 = (bf16[1024,512]{1,0:T(8,128)(2,1)S(1)}, bf16[1024,512]{1,0:T(8,128)(2,1)}, u32[]{:S(2)}) copy-start(bf16[1024,512]{1,0:T(8,128)(2,1)} %copy-done.2) | copy-start | bytes 3145732
Sparse Core Ops, SparseCore 0:
  9.2 532.3 all-gather.8
  634.9 302.1 all-reduce.2
  939.0 157.9 all-gather.4
  1098.7 159.1 all-gather.6
where the time goes:
time: 1290 us
  waiting for transfers between devices  1140 us (88%)
  blocking collectives  81.6 us (6%)
  matrix products  33.3 us (3%)
  between operations  13.2 us (1%)
    all_gather x1, waiting for transfers between devices, per_device(): lax.all_gather(batch_points, ('narrow', 'wide', 'nys'), axis=0, tiled=True)  524 us
    psum x1, waiting for transfers between devices, per_device(): projected = lax.psum(local_proj, ('narrow', 'nys'))  301 us
    all_gather x1, waiting for transfers between devices, per_device(): coefs = lax.all_gather(corrected, ('narrow', 'nys'), axis=0, tiled=True)  158 us
    all_gather x1, waiting for transfers between devices, per_device(): lax.all_gather(nystrom_points, ('narrow', 'nys'), axis=0, tiled=True)  158 us
    psum x1, blocking collectives, per_device(): lax.psum(partial_value - placed, ('narrow', 'wide', 'nys'))  81.6 us
  transfers between devices with their start and end apart: 4, of which 4 were waited for; matrix products, arithmetic and copies ran while one was open for 1% of the time, Pallas kernels for 0%

commit v1 on v0

--- a/solution.py
+++ b/solution.py
@@ -47,7 +47,8 @@
     local_proj = lax.dot_general(
         eigvecs, pulled, (((0,), (0,)), ((), ())), precision=lax.Precision.HIGHEST
     )
-    projected = lax.psum(local_proj, ("narrow", "nys"))
+    half = lax.psum(local_proj, "narrow")
+    projected = lax.psum(half, "nys")
     scaled_proj = corrections[:, None] * projected
     gradient = jnp.dot(k_batch, residual, preferred_element_type=jnp.float32)
     corrected = jnp.dot(eigvecs, scaled_proj, precision=lax.Precision.HIGHEST).astype(jnp.bfloat16)

time: 1290 us -> 1070 us (0.83)
  waiting for transfers between devices: 1140 us -> 921 us
    psum x1 -> x2, waiting for transfers between devices: 301 us -> 132 us  [the longest x1 80.1 us: per_device(): half = lax.psum(local_proj, 'narrow')]
    all_gather x1, waiting for transfers between devices: 158 us -> 106 us  [per_device(): lax.all_gather(nystrom_points, ('narrow', 'nys'), axis=0, tiled=True)]
  transfers between devices with their start and end apart: 4 -> 5, of which waited for: 4 -> 5; matrix products, arithmetic and copies ran while one was open for 1% -> 1% of each run, Pallas kernels for 0% -> 0%
where the time goes in v1:
time: 1070 us
  waiting for transfers between devices  921 us (86%)
  blocking collectives  81.6 us (8%)
  matrix products  33.3 us (3%)
  between operations  14.7 us (1%)
    all_gather x1, waiting for transfers between devices, per_device(): lax.all_gather(batch_points, ('narrow', 'wide', 'nys'), axis=0, tiled=True)  524 us
    all_gather x1, waiting for transfers between devices, per_device(): coefs = lax.all_gather(corrected, ('narrow', 'nys'), axis=0, tiled=True)  158 us
    all_gather x1, waiting for transfers between devices, per_device(): lax.all_gather(nystrom_points, ('narrow', 'nys'), axis=0, tiled=True)  106 us
    psum x1, blocking collectives, per_device(): lax.psum(partial_value - placed, ('narrow', 'wide', 'nys'))  81.6 us
    psum x1, waiting for transfers between devices, per_device(): half = lax.psum(local_proj, 'narrow')  80.1 us
    psum x1, waiting for transfers between devices, per_device(): projected = lax.psum(half, 'nys')  52.4 us
  transfers between devices with their start and end apart: 5, of which 5 were waited for; matrix products, arithmetic and copies ran while one was open for 1% of the time, Pallas kernels for 0%

profile of v1, /device:TPU:2, one launch (start us, length us, event | category | flops | bytes accessed | tf_op | source)
XLA Modules:
  0.0 1067.8 jit_solution(1380728799374887871)
XLA Ops:
  7.4 0.0 copy-start
  7.4 0.0 all-gather.9.cloned.1.call-start
  7.4 0.7 all-gather.9.cloned.1.call-update
  8.1 0.0 all-reduce.4.cloned.1.call-start
  8.1 0.9 copy.9
  9.1 0.2 broadcast_in_dim.2
  9.3 6.3 dynamic_update_slice.3
  15.6 1.0 multiply_reduce_fusion.3
  16.7 2.1 multiply_reduce_fusion.1
  18.7 523.6 %all-gather.9.cloned.1.call-done = bf16[256,2,1024]{2,1,0:T(2,128)(2,1)} async-done(((bf16[1,2,1024]{2,1,0:T(2,128)(2,1)}), bf16[256,2,1024]{2,1,0:T(2,128)(2,1)}) %all-gather.9.cloned.1.call-update) | async-done | bytes 1048592 | tf_op jit(solution)/shard_map/all_gather | solution.py:27
  542.3 1.5 reshape.6
  543.8 0.3 multiply_reduce_fusion.2
  544.1 0.0 copy-start.1
  544.1 3.8 exponential_convert_fusion.1
  547.9 0.0 copy-start.2
  547.9 1.1 copy-done.2
  549.0 0.0 copy-done.1
  549.0 0.0 copy-start.4
  549.0 2.6 multiply_subtract_fusion.1
  551.6 0.0 copy-start.5
  551.6 81.6 %all-reduce.7 = bf16[512,1000]{0,1:T(8,128)(2,1)S(1)} all-reduce(f32[512,1000]{0,1:T(8,128)} %multiply_subtract_fusion.1), channel_id=1, replica_groups=mesh['narrow'=8,'wide'=8,'nys'=4] {'narrow','wide','nys'}, use_global_device_ids=true, to_apply=%region_2.0 | all-reduce | flops 512000 | bytes 3072000 | tf_op jit(solution)/shard_map/psum | solution.py:44
  633.1 0.0 copy-done.4
  633.1 0.8 fusion.12
  634.0 0.0 copy-done
  634.0 1.6 convolution_bitcast_fusion
  635.5 0.0 all-reduce.4.cloned.1.call-update
  635.6 0.0 all-reduce.6.cloned.1.call-start
  635.6 80.1 %all-reduce.4.cloned.1.call-done = f32[160,1000]{1,0:T(8,128)} async-done(((f32[160,1000]{1,0:T(8,128)}), f32[160,1000]{1,0:T(8,128)}) %all-reduce.4.cloned.1.call-update) | async-done | bytes 640016 | tf_op jit(solution)/shard_map/psum | solution.py:50
  715.7 0.0 all-reduce.6.cloned.1.call-update
  715.7 0.0 all-gather.5.cloned.1.call-start
  715.8 0.5 all-gather.5.cloned.1.call-update
  716.3 0.2 all-gather.7.cloned.1.call-start
  716.5 52.4 %all-reduce.6.cloned.1.call-done = f32[160,1000]{1,0:T(8,128)} async-done(((f32[160,1000]{1,0:T(8,128)}), f32[160,1000]{1,0:T(8,128)}) %all-reduce.6.cloned.1.call-update) | async-done | bytes 640016 | tf_op jit(solution)/shard_map/psum | solution.py:51
  768.9 0.0 copy-done.5
  768.9 2.3 fusion.4
  771.2 0.0 all-gather.7.cloned.1.call-update
  771.3 105.7 %all-gather.5.cloned.1.call-done = bf16[2048,1024]{1,0:T(8,128)(2,1)} async-done(((bf16[64,1024]{1,0:T(8,128)(2,1)}), bf16[2048,1024]{1,0:T(8,128)(2,1)}) %all-gather.5.cloned.1.call-update) | async-done | bytes 4194320 | tf_op jit(solution)/shard_map/all_gather | solution.py:55
  876.9 3.1 multiply_reduce_fusion
  880.0 0.0 copy-start.3
  880.0 158.5 %all-gather.7.cloned.1.call-done = bf16[2048,1000]{1,0:T(8,128)(2,1)} async-done(((bf16[64,1000]{1,0:T(8,128)(2,1)}), bf16[2048,1000]{1,0:T(8,128)(2,1)}) %all-gather.7.cloned.1.call-update) | async-done | bytes 4096016 | tf_op jit(solution)/shard_map/all_gather | solution.py:56
  1038.5 15.5 %fusion.13 = f32[1024,1000]{0,1:T(8,128)} fusion(bf16[2048,1000]{1,0:T(8,128)(2,1)} %all-gather.7.cloned.1.call-done, bf16[1024,1024]{1,0:T(8,128)(2,1)} %param.7, bf16[2048,1024]{1,0:T(8,128)(2,1)} %all-gather.5.cloned.1.call-done, f32[2048]{0:T(1024)S(1)} %multiply_reduce_fusion, f32[1024]{0:T(1024)S(1)} %multiply_reduce_fusion.1), kind=kOutput, calls=%fused_computation.21 | convolution fusion | flops 8503951360 | bytes 14495744 | tf_op jit(solution)/shard_map/dot_general | solution.py:58
  1054.0 0.0 copy-done.3
  1054.0 6.7 multiply_subtract_fusion
Async XLA Ops:
  7.4 626.6 %copy-start = (f32[64,160]{1,0:T(8,128)S(1)}, f32[64,160]{1,0:T(8,128)}, u32[]{:S(2)}) copy-start(f32[64,160]{1,0:T(8,128)} %param.12) | copy-start | bytes 122884
  7.4 535.0 %all-gather.9.cloned.1.call-start = ((), (), s32[]{:S(2)}) async-start(), calls=%async_computation.4 | async-start | bytes 1052672 | tf_op jit(solution)/shard_map/all_gather | solution.py:27
  8.1 707.6 %all-reduce.4.cloned.1.call-start = ((), (), s32[]{:S(2)}) async-start(), calls=%async_computation.1 | async-start | bytes 1310720 | tf_op jit(solution)/shard_map/psum | solution.py:50
  544.1 4.9 copy-start.1
  547.9 1.1 copy-start.2
  549.0 84.1 %copy-start.4 = (bf16[64,1024]{1,0:T(8,128)(2,1)S(1)}, bf16[64,1024]{1,0:T(8,128)(2,1)}, u32[]{:S(2)}) copy-start(bf16[64,1024]{1,0:T(8,128)(2,1)} %param.11) | copy-start | bytes 393220
  551.6 217.3 %copy-start.5 = (f32[160]{0:T(256)S(1)}, f32[160]{0:T(256)}, u32[]{:S(2)}) copy-start(f32[160]{0:T(256)} %param.13) | copy-start | bytes 1924
  635.6 133.3 %all-reduce.6.cloned.1.call-start = ((), (), s32[]{:S(2)}) async-start(), calls=%async_computation.2 | async-start | bytes 1310720 | tf_op jit(solution)/shard_map/psum | solution.py:51
  715.7 161.2 %all-gather.5.cloned.1.call-start = ((), (), s32[]{:S(2)}) async-start(), calls=%async_computation | async-start | bytes 4325376 | tf_op jit(solution)/shard_map/all_gather | solution.py:55
  716.3 322.2 %all-gather.7.cloned.1.call-start = ((), (), s32[]{:S(2)}) async-start(), calls=%async_computation.3 | async-start | bytes 4325376 | tf_op jit(solution)/shard_map/all_gather | solution.py:56
  880.0 174.0 %copy-start.3 = (bf16[1024,512]{1,0:T(8,128)(2,1)S(1)}, bf16[1024,512]{1,0:T(8,128)(2,1)}, u32[]{:S(2)}) copy-start(bf16[1024,512]{1,0:T(8,128)(2,1)} %copy-done.2) | copy-start | bytes 3145732
Sparse Core Ops, SparseCore 0:
  10.0 532.3 all-gather.8
  635.7 79.9 all-reduce.3
  718.0 50.8 all-reduce.5
Sparse Core Ops, SparseCore 1:
  718.0 158.9 all-gather.4
  878.6 159.9 all-gather.6

commit v2 on v0

--- a/solution.py
+++ b/solution.py
@@ -3,6 +3,7 @@
 import jax.numpy as jnp
 from jax import lax
 from jax.sharding import PartitionSpec as P
+from jax.lax import all_gather
 
 BATCH = 512
 RATE = 16.0
@@ -51,8 +52,10 @@
     scaled_proj = corrections[:, None] * projected
     gradient = jnp.dot(k_batch, residual, preferred_element_type=jnp.float32)
     corrected = jnp.dot(eigvecs, scaled_proj, precision=lax.Precision.HIGHEST).astype(jnp.bfloat16)
-    points = lax.all_gather(nystrom_points, ("narrow", "nys"), axis=0, tiled=True)
-    coefs = lax.all_gather(corrected, ("narrow", "nys"), axis=0, tiled=True)
+    fresh = jnp.concatenate([nystrom_points, corrected], axis=1)
+    points, coefs = jnp.split(
+        all_gather(fresh, ("narrow", "nys"), tiled=True, axis=0), [nystrom_points.shape[1]], axis=1
+    )
     tile = kernel_with(centers, center_sq, points)
     nystrom_term = jnp.dot(tile, coefs, preferred_element_type=jnp.float32)
     return weights - RATE / BATCH * (gradient - nystrom_term)

time: 1290 us -> 1140 us (0.88)
  waiting for transfers between devices: 1140 us -> 996 us
    all_gather x2 -> x1, waiting for transfers between devices: 315 us -> 169 us  [per_device(): all_gather(fresh, ('narrow', 'nys'), tiled=True, axis=0)]
  transfers between devices with their start and end apart: 4 -> 3, of which waited for: 4 -> 3; matrix products, arithmetic and copies ran while one was open for 1% -> 1% of each run, Pallas kernels for 0% -> 0%
where the time goes in v2:
time: 1140 us
  waiting for transfers between devices  996 us (87%)
  blocking collectives  81.6 us (7%)
  matrix products  32.6 us (3%)
  between operations  13.2 us (1%)
    all_gather x1, waiting for transfers between devices, per_device(): lax.all_gather(batch_points, ('narrow', 'wide', 'nys'), axis=0, tiled=True)  524 us
    psum x1, waiting for transfers between devices, per_device(): projected = lax.psum(local_proj, ('narrow', 'nys'))  302 us
    all_gather x1, waiting for transfers between devices, per_device(): all_gather(fresh, ('narrow', 'nys'), tiled=True, axis=0)  169 us
    psum x1, blocking collectives, per_device(): lax.psum(partial_value - placed, ('narrow', 'wide', 'nys'))  81.6 us
  transfers between devices with their start and end apart: 3, of which 3 were waited for; matrix products, arithmetic and copies ran while one was open for 1% of the time, Pallas kernels for 0%

profile of v2, /device:TPU:2, one launch (start us, length us, event | category | flops | bytes accessed | tf_op | source)
XLA Modules:
  0.0 1140.5 jit_solution(4068086824592146472)
XLA Ops:
  6.5 0.0 copy-start
  6.5 0.0 all-gather.6.cloned.1.call-start
  6.5 0.7 all-gather.6.cloned.1.call-update
  7.3 0.0 all-reduce.3.cloned.1.call-start
  7.3 0.9 copy.9
  8.2 0.2 broadcast_in_dim.2
  8.5 6.3 dynamic_update_slice.3
  14.8 1.0 multiply_reduce_fusion.3
  15.8 2.1 multiply_reduce_fusion.1
  17.9 523.6 %all-gather.6.cloned.1.call-done = bf16[256,2,1024]{2,1,0:T(2,128)(2,1)} async-done(((bf16[1,2,1024]{2,1,0:T(2,128)(2,1)}), bf16[256,2,1024]{2,1,0:T(2,128)(2,1)}) %all-gather.6.cloned.1.call-update) | async-done | bytes 1048592 | tf_op jit(solution)/shard_map/all_gather | solution.py:28
  541.5 1.5 reshape.6
  543.0 0.3 multiply_reduce_fusion.2
  543.3 0.0 copy-start.1
  543.3 3.8 exponential_convert_fusion
  547.1 0.0 copy-start.2
  547.1 1.1 copy-done.2
  548.2 0.0 copy-done.1
  548.2 0.0 copy-start.4
  548.2 2.6 multiply_subtract_fusion.1
  550.7 0.0 copy-start.5
  550.7 81.6 %all-reduce.4 = bf16[512,1000]{0,1:T(8,128)(2,1)S(1)} all-reduce(f32[512,1000]{0,1:T(8,128)} %multiply_subtract_fusion.1), channel_id=1, replica_groups=mesh['narrow'=8,'wide'=8,'nys'=4] {'narrow','wide','nys'}, use_global_device_ids=true, to_apply=%region_2.0 | all-reduce | flops 512000 | bytes 3072000 | tf_op jit(solution)/shard_map/psum | solution.py:45
  632.3 0.0 copy-done.4
  632.3 0.8 fusion.23
  633.2 0.0 copy-done
  633.2 1.6 convolution_bitcast_fusion
  634.7 0.0 all-reduce.3.cloned.1.call-update
  634.7 0.2 all-gather.4.cloned.1.call-start
  635.0 302.3 %all-reduce.3.cloned.1.call-done = f32[160,1000]{1,0:T(8,128)} async-done(((f32[160,1000]{1,0:T(8,128)}), f32[160,1000]{1,0:T(8,128)}) %all-reduce.3.cloned.1.call-update) | async-done | bytes 640016 | tf_op jit(solution)/shard_map/psum | solution.py:51
  937.3 0.0 copy-done.5
  937.3 1.7 fusion.15
  939.0 0.7 pad_maximum_fusion
  939.7 0.0 all-gather.4.cloned.1.call-update
  939.8 169.0 %all-gather.4.cloned.1.call-done = bf16[2048,2024]{1,0:T(8,128)(2,1)} async-done(((bf16[64,2024]{1,0:T(8,128)(2,1)}), bf16[2048,2024]{1,0:T(8,128)(2,1)}) %all-gather.4.cloned.1.call-update) | async-done | bytes 8290320 | tf_op jit(solution)/shard_map/all_gather | solution.py:57
  1108.7 3.1 multiply_reduce_fusion
  1111.8 0.0 copy-start.3
  1111.8 15.5 %fusion.6 = f32[1024,1000]{0,1:T(8,128)} fusion(bf16[2048,2024]{1,0:T(8,128)(2,1)} %all-gather.4.cloned.1.call-done, bf16[1024,1024]{1,0:T(8,128)(2,1)} %param.7, f32[2048]{0:T(1024)S(1)} %multiply_reduce_fusion, f32[1024]{0:T(1024)S(1)} %multiply_reduce_fusion.1), kind=kOutput, calls=%fused_computation.8 | convolution fusion | flops 8503951360 | bytes 14495744 | tf_op jit(solution)/shard_map/dot_general | solution.py:60
  1127.3 0.0 copy-done.3
  1127.4 6.7 multiply_subtract_fusion
Async XLA Ops:
  6.5 626.6 %copy-start = (f32[64,160]{1,0:T(8,128)S(1)}, f32[64,160]{1,0:T(8,128)}, u32[]{:S(2)}) copy-start(f32[64,160]{1,0:T(8,128)} %param.12) | copy-start | bytes 122884
  6.5 535.0 %all-gather.6.cloned.1.call-start = ((), (), s32[]{:S(2)}) async-start(), calls=%async_computation.2 | async-start | bytes 1052672 | tf_op jit(solution)/shard_map/all_gather | solution.py:28
  7.3 930.1 %all-reduce.3.cloned.1.call-start = ((), (), s32[]{:S(2)}) async-start(), calls=%async_computation | async-start | bytes 1310720 | tf_op jit(solution)/shard_map/psum | solution.py:51
  543.3 4.9 copy-start.1
  547.1 1.1 copy-start.2
  548.2 84.1 %copy-start.4 = (bf16[64,1024]{1,0:T(8,128)(2,1)S(1)}, bf16[64,1024]{1,0:T(8,128)(2,1)}, u32[]{:S(2)}) copy-start(bf16[64,1024]{1,0:T(8,128)(2,1)} %param.11) | copy-start | bytes 393220
  550.7 386.6 %copy-start.5 = (f32[160]{0:T(256)S(1)}, f32[160]{0:T(256)}, u32[]{:S(2)}) copy-start(f32[160]{0:T(256)} %param.13) | copy-start | bytes 1924
  634.7 474.0 %all-gather.4.cloned.1.call-start = ((), (), s32[]{:S(2)}) async-start(), calls=%async_computation.1 | async-start | bytes 8650752 | tf_op jit(solution)/shard_map/all_gather | solution.py:57
  1111.8 15.6 %copy-start.3 = (bf16[1024,512]{1,0:T(8,128)(2,1)S(1)}, bf16[1024,512]{1,0:T(8,128)(2,1)}, u32[]{:S(2)}) copy-start(bf16[1024,512]{1,0:T(8,128)(2,1)} %copy-done.2) | copy-start | bytes 3145732
Sparse Core Ops, SparseCore 0:
  9.2 532.3 all-gather.5
  634.9 302.4 all-reduce.2
  939.9 168.8 all-gather.3
